TPU v7x, 512 devices: a whole 4x4x16 slice. The times are simulated.
512 devices in a mesh: seq: 32 (over z_hi, y, core), section: 16 (over z_lo, x).
Axes of the slice: x: 4, y: 4, z: 16 (z_hi: 4, z_lo: 4; z = z_hi * 4 + z_lo), core: 2. Of those that a mesh axis runs over, the one named last changes fastest.
Arguments:
- queries: bfloat16 [16, 2, 4096, 2048], P('section', None, 'seq'), may hold values from -120 to 120
- keys: bfloat16 [16, 2, 4096, 1024], P('section', None, 'seq'), may hold values from -4 to 4
- values: bfloat16 [16, 2, 4096, 1024], P('section', None, 'seq'), may hold values from -8 to 8
- out_grad: bfloat16 [16, 4096, 2048], P('section', 'seq'), may hold values from -6 to 6
- segments: int32 [2, 4096], replicated, may hold values from 0 to 3, never falling along the last dimension, each value on 1 to 2048 neighbouring positions
Outputs:
- attended: bfloat16 [16, 4096, 2048], P('section', 'seq')
- grad_queries: bfloat16 [16, 4096, 2048], P('section', 'seq')
- grad_keys: bfloat16 [16, 4096, 1024], P('section', 'seq')
- grad_values: bfloat16 [16, 4096, 1024], P('section', 'seq')
Inputs may be any that keep to these rules, and one draw needn't show every extreme that they name: `segments`: documents are numbered in order along each micro-batch.
All inputs are finite; a program needn't handle non-finite values.
Results may differ from a plain program's by a relative error of at most 0.033.
Values may be sent and summed in bfloat16 or wider, within the bound.
A program may use at most 64 MiB of HBM per device.

v0:
```python
import jax
import jax.numpy as jnp
from jax import lax
from jax.sharding import PartitionSpec as P

QHEADS = 16
KVHEADS = 8
HEAD_DIM = 128
WINDOW = 256


score_scale = 168.0 ** (-0.5)
masked_score = -1e30


def from_behind(value, axis, steps):
    count = lax.axis_size(axis)
    initial, last = (max(0, -steps), min(count, count - steps))
    return lax.ppermute(value, axis, [(source, source + steps) for source in range(initial, last)])


def shifted(block, axis, distance):
    devices = range(lax.axis_size(axis))
    route = [((i - distance) % len(devices), i) for i in devices]
    return lax.ppermute(block, axis, route)


def masked_probs(query_block, key_span, kv_count, seg_query, seg_key, query_pos, key_pos):
    row_count = query_block.shape[0]
    span_rows = key_span.shape[0]
    queries_grouped = query_block.reshape(row_count, kv_count, QHEADS // KVHEADS, HEAD_DIM)
    keys_grouped = key_span.reshape(span_rows, kv_count, HEAD_DIM)
    scores = (
        jnp.einsum(
            "rkgd,lkd->kgrl", queries_grouped, keys_grouped, preferred_element_type=jnp.float32
        )
        * score_scale
    )
    offset = query_pos[:, None] - key_pos[None, :]
    allowed = (seg_query[:, None] == seg_key[None, :]) & (offset >= 0) & (offset < WINDOW)
    scores = jnp.where(allowed, scores, masked_score)
    highest = jnp.max(scores, axis=-1, keepdims=True)
    weights = jnp.exp(scores - highest)
    return weights / jnp.sum(weights, axis=-1, keepdims=True)


def halo_layer(queries, keys, values, out_grad, segments):
    row_count = queries.shape[2]
    block_count = WINDOW // row_count
    span_rows = WINDOW + row_count
    groups = QHEADS // KVHEADS
    row_start = lax.axis_index("seq") * row_count
    own_pair = (keys[0], values[0])
    pieces = []
    for distance in range(1, block_count + 1):
        pieces.append(from_behind((own_pair[0], own_pair[1]), "seq", distance))
    ordered = pieces[::-1]
    key_span = jnp.concatenate([received[0] for received in ordered] + [keys[0]], axis=1)
    value_span = jnp.concatenate([received[1] for received in ordered] + [values[0]], axis=1)
    query_pos = row_start + jnp.arange(row_count, dtype=jnp.int32)
    key_pos = row_start - WINDOW + jnp.arange(span_rows, dtype=jnp.int32)
    seg_padded = jnp.concatenate([jnp.full((2, WINDOW), -1, jnp.int32), segments], axis=1)
    seg_key = lax.dynamic_slice_in_dim(seg_padded, row_start, span_rows, 1)
    seg_query = lax.dynamic_slice_in_dim(segments, row_start, row_count, 1)
    values_grouped = value_span.reshape(2, span_rows, KVHEADS, HEAD_DIM)
    keys_grouped = key_span.reshape(2, span_rows, KVHEADS, HEAD_DIM)
    forward_probs = masked_probs(
        queries[0, 0], key_span[0], KVHEADS, seg_query[0], seg_key[0], query_pos, key_pos
    ).astype(jnp.bfloat16)
    attended = jnp.einsum(
        "kgrl,lkd->rkgd", forward_probs, values_grouped[0], preferred_element_type=jnp.float32
    )
    attended = attended.reshape(row_count, QHEADS * HEAD_DIM).astype(jnp.bfloat16)
    back_probs = masked_probs(
        queries[0, 1], key_span[1], KVHEADS, seg_query[1], seg_key[1], query_pos, key_pos
    )
    back_half = back_probs.astype(jnp.bfloat16)
    recomputed = jnp.einsum(
        "kgrl,lkd->rkgd", back_half, values_grouped[1], preferred_element_type=jnp.float32
    ).astype(jnp.bfloat16)
    grad_grouped = out_grad[0].reshape(row_count, KVHEADS, groups, HEAD_DIM)
    grad_probs = jnp.einsum(
        "rkgd,lkd->kgrl", grad_grouped, values_grouped[1], preferred_element_type=jnp.float32
    )
    row_delta = jnp.sum(
        grad_grouped.astype(jnp.float32) * recomputed.astype(jnp.float32), axis=-1
    ).transpose(1, 2, 0)
    grad_scores = (score_scale * back_probs * (grad_probs - row_delta[..., None])).astype(
        jnp.bfloat16
    )
    query_grad = jnp.einsum(
        "kgrl,lkd->rkgd", grad_scores, keys_grouped[1], preferred_element_type=jnp.float32
    )
    query_grad = query_grad.reshape(row_count, QHEADS * HEAD_DIM).astype(jnp.bfloat16)
    back_queries = queries[0, 1].reshape(row_count, KVHEADS, groups, HEAD_DIM)
    key_terms = jnp.einsum(
        "kgrl,rkgd->lkd", grad_scores, back_queries, preferred_element_type=jnp.float32
    ).reshape(span_rows, KVHEADS * HEAD_DIM)
    value_terms = jnp.einsum(
        "kgrl,rkgd->lkd", back_half, grad_grouped, preferred_element_type=jnp.float32
    ).reshape(span_rows, KVHEADS * HEAD_DIM)
    remote_terms = jnp.stack([key_terms[:WINDOW], value_terms[:WINDOW]]).astype(jnp.bfloat16)
    summed = jnp.stack([key_terms[WINDOW:], value_terms[WINDOW:]])
    for distance in range(1, block_count + 1):
        first_row = (block_count - distance) * row_count
        outgoing = remote_terms[:, first_row : first_row + row_count]
        summed = summed + from_behind(outgoing, "seq", -distance).astype(jnp.float32)
    return (attended, query_grad, summed[0].astype(jnp.bfloat16), summed[1].astype(jnp.bfloat16))


def shards(queries, keys, values, out_grad, segments):
    attended, query_grad, key_grad, value_grad = halo_layer(
        queries, keys, values, out_grad, segments
    )
    forward_out = shifted(attended[None], "section", 1)
    grad_queries, grad_keys, grad_values = shifted(
        (query_grad[None], key_grad[None], value_grad[None]), "section", -1
    )
    return (forward_out, grad_queries, grad_keys, grad_values)


def solution(mesh):
    return jax.shard_map(
        shards,
        mesh=mesh,
        in_specs=(
            P("section", None, "seq", None),
            P("section", None, "seq", None),
            P("section", None, "seq", None),
            P("section", "seq", None),
            P(),
        ),
        out_specs=(
            P("section", "seq", None),
            P("section", "seq", None),
            P("section", "seq", None),
            P("section", "seq", None),
        ),
        check_vma=False,
    )
```

profile of v0, /device:TPU:199, one launch (start us, length us, event | category | flops | bytes accessed | tf_op | source)
XLA Modules:
  0.0 225.9 jit_solution(3068671070613897302)
XLA Ops:
  0.6 0.0 copy-start.5
  0.6 0.0 copy-start.4
  0.7 1.4 copy.26
  2.0 3.8 %collective-permute-start.1 = (bf16[2,128,1024]{1,2,0:T(8,128)(2,1)S(1)}, bf16[2,128,1024]{1,2,0:T(8,128)(2,1)}, u32[]{:S(2)}, u32[]{:S(2)}) collective-permute-start(bf16[2,128,1024]{1,2,0:T(8,128)(2,1)S(1)} %bitcast.118), channel_id=1, source_target_pairs={{0,16},{16,32},{32,48},{48,64},{64,80},{80,96},{96,112},{112,128},... | collective-permute-start | bytes 1572872 | tf_op jit(solution)/shard_map/ppermute | solution.py:19
  5.8 3.2 %collective-permute-start = (bf16[2,128,1024]{1,2,0:T(8,128)(2,1)S(1)}, bf16[2,128,1024]{1,2,0:T(8,128)(2,1)}, u32[]{:S(2)}, u32[]{:S(2)}) collective-permute-start(bf16[2,128,1024]{1,2,0:T(8,128)(2,1)S(1)} %bitcast.119), channel_id=1, source_target_pairs={{0,32},{16,48},{32,64},{48,80},{64,96},{80,112},{96,128},{112,144}... | collective-permute-start | bytes 1572872 | tf_op jit(solution)/shard_map/ppermute | solution.py:19
  9.0 1.3 copy.27
  10.3 2.2 collective-permute-start.3
  12.5 2.9 %collective-permute-start.2 = (bf16[2,128,1024]{1,2,0:T(8,128)(2,1)S(1)}, bf16[2,128,1024]{1,2,0:T(8,128)(2,1)}, u32[]{:S(2)}, u32[]{:S(2)}) collective-permute-start(bf16[2,128,1024]{1,2,0:T(8,128)(2,1)S(1)} %bitcast.116), channel_id=1, source_target_pairs={{0,32},{16,48},{32,64},{48,80},{64,96},{80,112},{96,128},{112,144}... | collective-permute-start | bytes 1572872 | tf_op jit(solution)/shard_map/ppermute | solution.py:19
  15.5 1.3 fusion.40
  16.8 0.0 copy-done.5
  16.8 0.1 fusion.31
  16.9 0.2 fusion.24
  17.1 1.0 copy.70
  18.1 0.0 copy-done.4
  18.1 0.3 copy.36
  18.4 0.3 copy.71
  18.7 0.0 copy-start.2
  18.7 0.0 collective-permute-done.1
  18.7 83.6 %collective-permute-done = bf16[2,128,1024]{1,2,0:T(8,128)(2,1)} collective-permute-done((bf16[2,128,1024]{1,2,0:T(8,128)(2,1)S(1)}, bf16[2,128,1024]{1,2,0:T(8,128)(2,1)}, u32[]{:S(2)}, u32[]{:S(2)}) %collective-permute-start) | collective-permute-done | bytes 524320 | tf_op jit(solution)/shard_map/ppermute | solution.py:19
  102.3 1.4 pad_maximum_fusion
  103.7 1.1 fusion.38
  104.8 0.0 collective-permute-done.3
  104.8 8.7 %collective-permute-done.2 = bf16[2,128,1024]{1,2,0:T(8,128)(2,1)} collective-permute-done((bf16[2,128,1024]{1,2,0:T(8,128)(2,1)S(1)}, bf16[2,128,1024]{1,2,0:T(8,128)(2,1)}, u32[]{:S(2)}, u32[]{:S(2)}) %collective-permute-start.2) | collective-permute-done | bytes 524320 | tf_op jit(solution)/shard_map/ppermute | solution.py:19
  113.4 1.4 pad_maximum_fusion.1
  114.8 1.2 fusion.39
  116.0 0.0 copy-done.2
  116.0 2.8 %fusion.43 = (f32[8,2,128]{2,1,0:T(2,128)S(1)}, f32[8,2,128,384]{2,3,1,0:T(8,128)}) fusion(pred[128,384]{0,1:T(8,128)(4,1)S(1)} %get-tuple-element.16, bf16[384,8,128,1]{0,2,3,1:T(8,128)(2,1)S(1)} %bitcast.108, bf16[128,8,2,128]{0,3,2,1:T(8,128)(2,1)S(1)} %bitcast.110), kind=kOutput, calls=%fused_computation.67 | convolution fusion | flops 204472704 | bytes 4513792 | tf_op jit(solution)/shard_map/sub | solution.py:43
  118.8 0.0 copy-done.1
  118.8 3.8 %convolution_bitcast_fusion = f32[384,8,128]{0,2,1:T(8,128)} fusion(bf16[128,8,2,128]{0,3,2,1:T(8,128)(2,1)S(1)} %bitcast.127, f32[8,2,128,384]{2,3,1,0:T(8,128)} %get-tuple-element.23, f32[8,2,128]{2,1,0:T(2,128)S(1)} %get-tuple-element.22), kind=kOutput, calls=%fused_computation.22 | convolution fusion | flops 202899456 | bytes 5251072 | tf_op jit(solution)/shard_map/kgrl,rkgd->lkd/dot_general | solution.py:99
  122.6 0.5 fusion.18
  123.1 0.0 copy-start.3
  123.1 0.9 fusion.3
  124.0 0.1 copy-done.3
  124.1 0.6 convolution_bitcast_fusion.1
  124.7 0.9 slice.109
  125.6 2.0 copy.46
  127.7 2.1 slice.108
  129.8 2.0 copy.47
  131.8 2.3 %fusion.21 = (bf16[2,128,1024]{2,1,0:T(8,128)(2,1)}, bf16[2,128,1024]{2,1,0:T(8,128)(2,1)}) fusion(bf16[1,256,1024]{2,1,0:T(8,128)(2,1)} %copy.46, bf16[1,256,1024]{2,1,0:T(8,128)(2,1)} %copy.47), kind=kLoop, calls=%fused_computation.39 | loop fusion | flops 2097152 | bytes 2097152 | tf_op jit(solution)/shard_map/stack | solution.py:102
  134.1 1.9 collective-permute-start.7
  136.0 1.9 collective-permute-start.6
  138.0 4.1 %fusion.42 = (f32[8,2,128]{2,1,0:T(2,128)S(1)}, f32[8,2,128,384]{2,3,1,0:T(8,128)}) fusion(pred[128,384]{0,1:T(8,128)(4,1)S(1)} %get-tuple-element.17, bf16[384,8,128,1]{0,2,3,1:T(8,128)(2,1)} %bitcast.123, bf16[128,8,2,128]{0,3,2,1:T(8,128)(2,1)} %bitcast.126), kind=kOutput, calls=%fused_computation.66 | convolution fusion | flops 204472704 | bytes 4513792 | tf_op jit(solution)/shard_map/sub | solution.py:43
  142.0 3.4 %fusion.13 = bf16[8,128,2,128]{3,1,2,0:T(8,128)(2,1)} fusion(bf16[384,8,128,1]{0,2,3,1:T(8,128)(2,1)} %bitcast.122, f32[8,2,128,384]{2,3,1,0:T(8,128)} %get-tuple-element.21, f32[8,2,128]{2,1,0:T(2,128)S(1)} %get-tuple-element.20), kind=kOutput, calls=%fused_computation.24 | convolution fusion | flops 203161600 | bytes 4464640 | tf_op jit(solution)/shard_map/kgrl,lkd->rkgd/dot_general | solution.py:70
  145.4 2.1 copy.32
  147.6 36.6 %collective-permute-start.4 = (bf16[1,128,2048]{2,1,0:T(8,128)(2,1)}, bf16[1,128,2048]{2,1,0:T(8,128)(2,1)}, u32[]{:S(2)}, u32[]{:S(2)}) collective-permute-start(bf16[1,128,2048]{2,1,0:T(8,128)(2,1)} %copy.32), channel_id=1, source_target_pairs={{15,0},{0,1},{1,2},{2,3},{3,4},{4,5},{5,6},{6,7},{7,8},{8,9},{9,10... | collective-permute-start | bytes 1572872 | tf_op jit(solution)/shard_map/ppermute | solution.py:25
  184.2 1.6 convolution_convert_fusion
  185.8 1.0 copy.41
  186.8 1.9 collective-permute-start.5
  188.7 0.2 copy.45
  188.9 0.0 slice-done
  188.9 0.2 copy.44
  189.1 0.0 collective-permute-done.7
  189.1 0.0 collective-permute-done.6
  189.1 1.4 fusion.20
  190.6 1.9 collective-permute-start.8
  192.5 1.9 collective-permute-start.9
  194.5 1.5 collective-permute-done.4
  196.0 14.6 %collective-permute-done.5 = bf16[1,128,2048]{2,1,0:T(8,128)(2,1)S(1)} collective-permute-done((bf16[1,128,2048]{2,1,0:T(8,128)(2,1)}, bf16[1,128,2048]{2,1,0:T(8,128)(2,1)S(1)}, u32[]{:S(2)}, u32[]{:S(2)}) %collective-permute-start.5) | collective-permute-done | bytes 524320 | tf_op jit(solution)/shard_map/ppermute | solution.py:25
  210.5 5.6 %collective-permute-done.8 = bf16[1,128,1024]{2,1,0:T(8,128)(2,1)S(1)} collective-permute-done((bf16[1,128,1024]{2,1,0:T(8,128)(2,1)S(1)}, bf16[1,128,1024]{2,1,0:T(8,128)(2,1)S(1)}, u32[]{:S(2)}, u32[]{:S(2)}) %collective-permute-start.8) | collective-permute-done | bytes 262176 | tf_op jit(solution)/shard_map/ppermute | solution.py:25
  216.2 5.6 %collective-permute-done.9 = bf16[1,128,1024]{2,1,0:T(8,128)(2,1)S(1)} collective-permute-done((bf16[1,128,1024]{2,1,0:T(8,128)(2,1)S(1)}, bf16[1,128,1024]{2,1,0:T(8,128)(2,1)S(1)}, u32[]{:S(2)}, u32[]{:S(2)}) %collective-permute-start.9) | collective-permute-done | bytes 262176 | tf_op jit(solution)/shard_map/ppermute | solution.py:25
  221.8 1.9 copy.76
  223.7 0.8 copy.77
  224.5 0.7 copy.78
  225.2 0.7 copy.79
  (13 shorter events, 0.1 us)
Async XLA Ops:
  0.6 16.1 %copy-start.5 = (s32[2,4096]{1,0:T(2,128)S(1)}, s32[2,4096]{1,0:T(2,128)}, u32[]{:S(2)}) copy-start(s32[2,4096]{1,0:T(2,128)} %param.9) | copy-start | bytes 98308
  0.6 17.5 %copy-start.4 = (bf16[1,128,2048]{2,1,0:T(8,128)(2,1)S(1)}, bf16[1,128,2048]{2,1,0:T(8,128)(2,1)}, u32[]{:S(2)}) copy-start(bf16[1,128,2048]{2,1,0:T(8,128)(2,1)} %param.8) | copy-start | bytes 1572868
  2.0 16.7 %collective-permute-start.1 = (bf16[2,128,1024]{1,2,0:T(8,128)(2,1)S(1)}, bf16[2,128,1024]{1,2,0:T(8,128)(2,1)}, u32[]{:S(2)}, u32[]{:S(2)}) collective-permute-start(bf16[2,128,1024]{1,2,0:T(8,128)(2,1)S(1)} %bitcast.118), channel_id=1, source_target_pairs={{0,16},{16,32},{32,48},{48,64},{64,80},{80,96},{96,112},{112,128},... | collective-permute-start | bytes 1572872 | tf_op jit(solution)/shard_map/ppermute | solution.py:19
  5.8 96.5 %collective-permute-start = (bf16[2,128,1024]{1,2,0:T(8,128)(2,1)S(1)}, bf16[2,128,1024]{1,2,0:T(8,128)(2,1)}, u32[]{:S(2)}, u32[]{:S(2)}) collective-permute-start(bf16[2,128,1024]{1,2,0:T(8,128)(2,1)S(1)} %bitcast.119), channel_id=1, source_target_pairs={{0,32},{16,48},{32,64},{48,80},{64,96},{80,112},{96,128},{112,144}... | collective-permute-start | bytes 1572872 | tf_op jit(solution)/shard_map/ppermute | solution.py:19
  10.3 94.4 %collective-permute-start.3 = (bf16[2,128,1024]{1,2,0:T(8,128)(2,1)S(1)}, bf16[2,128,1024]{1,2,0:T(8,128)(2,1)}, u32[]{:S(2)}, u32[]{:S(2)}) collective-permute-start(bf16[2,128,1024]{1,2,0:T(8,128)(2,1)S(1)} %bitcast.115), channel_id=1, source_target_pairs={{0,16},{16,32},{32,48},{48,64},{64,80},{80,96},{96,112},{112,128},... | collective-permute-start | bytes 1572872 | tf_op jit(solution)/shard_map/ppermute | solution.py:19
  12.5 100.9 %collective-permute-start.2 = (bf16[2,128,1024]{1,2,0:T(8,128)(2,1)S(1)}, bf16[2,128,1024]{1,2,0:T(8,128)(2,1)}, u32[]{:S(2)}, u32[]{:S(2)}) collective-permute-start(bf16[2,128,1024]{1,2,0:T(8,128)(2,1)S(1)} %bitcast.116), channel_id=1, source_target_pairs={{0,32},{16,48},{32,64},{48,80},{64,96},{80,112},{96,128},{112,144}... | collective-permute-start | bytes 1572872 | tf_op jit(solution)/shard_map/ppermute | solution.py:19
  18.7 97.3 %copy-start.2 = (bf16[1,1,128,2048]{2,3,1,0:T(8,128)(2,1)}, bf16[1,1,128,2048]{2,3,1,0:T(8,128)(2,1)S(1)}, u32[]{:S(2)}) copy-start(bf16[1,1,128,2048]{2,3,1,0:T(8,128)(2,1)S(1)} %copy.71) | copy-start | bytes 1572868
  116.0 2.8 %copy-start.1 = (bf16[1,384,1024]{1,2,0:T(8,128)(2,1)}, bf16[1,384,1024]{1,2,0:T(8,128)(2,1)S(1)}, u32[]{:S(2)}) copy-start(bf16[1,384,1024]{1,2,0:T(8,128)(2,1)S(1)} %get-tuple-element.8) | copy-start | bytes 2359300
  118.8 3.8 %copy-start.6 = (f32[8,2,128,384]{2,3,1,0:T(8,128)S(1)}, f32[8,2,128,384]{2,3,1,0:T(8,128)}, u32[]{:S(2)}) copy-start(f32[8,2,128,384]{2,3,1,0:T(8,128)} %get-tuple-element.23) | copy-start | bytes 9437188
  123.1 1.0 copy-start.3
  124.7 20.7 %copy-start = (f32[384,8,128]{0,2,1:T(8,128)}, f32[384,8,128]{0,2,1:T(8,128)S(1)}, u32[]{:S(2)}) copy-start(f32[384,8,128]{0,2,1:T(8,128)S(1)} %convolution_bitcast_fusion.1) | copy-start | bytes 4718596
  134.1 55.0 %collective-permute-start.7 = (bf16[2,128,1024]{2,1,0:T(8,128)(2,1)}, bf16[2,128,1024]{2,1,0:T(8,128)(2,1)}, u32[]{:S(2)}, u32[]{:S(2)}) collective-permute-start(bf16[2,128,1024]{2,1,0:T(8,128)(2,1)} %get-tuple-element.11), channel_id=1, source_target_pairs={{32,0},{48,16},{64,32},{80,48},{96,64},{112,80},{128,96},{144,112}... | collective-permute-start | bytes 1572872 | tf_op jit(solution)/shard_map/ppermute | solution.py:19
  136.0 53.1 %collective-permute-start.6 = (bf16[2,128,1024]{2,1,0:T(8,128)(2,1)}, bf16[2,128,1024]{2,1,0:T(8,128)(2,1)}, u32[]{:S(2)}, u32[]{:S(2)}) collective-permute-start(bf16[2,128,1024]{2,1,0:T(8,128)(2,1)} %get-tuple-element.10), channel_id=1, source_target_pairs={{16,0},{32,16},{48,32},{64,48},{80,64},{96,80},{112,96},{128,112},... | collective-permute-start | bytes 1572872 | tf_op jit(solution)/shard_map/ppermute | solution.py:19
  145.4 43.3 %slice-start.1 = ((f32[384,8,128]{0,2,1:T(8,128)}), f32[128,8,128]{0,2,1:T(8,128)S(1)}, s32[]{:S(2)}) async-start(f32[384,8,128]{0,2,1:T(8,128)} %convolution_bitcast_fusion), calls=%async_computation.1 | async-start | bytes 1048576 | tf_op jit(solution)/shard_map/slice | solution.py:103
  145.4 43.5 %slice-start = ((f32[384,8,128]{0,2,1:T(8,128)}), f32[128,8,128]{0,2,1:T(8,128)S(1)}, s32[]{:S(2)}) async-start(f32[384,8,128]{0,2,1:T(8,128)} %copy-done), calls=%async_computation | async-start | bytes 1048576 | tf_op jit(solution)/shard_map/slice | solution.py:103
  147.6 48.4 %collective-permute-start.4 = (bf16[1,128,2048]{2,1,0:T(8,128)(2,1)}, bf16[1,128,2048]{2,1,0:T(8,128)(2,1)}, u32[]{:S(2)}, u32[]{:S(2)}) collective-permute-start(bf16[1,128,2048]{2,1,0:T(8,128)(2,1)} %copy.32), channel_id=1, source_target_pairs={{15,0},{0,1},{1,2},{2,3},{3,4},{4,5},{5,6},{6,7},{7,8},{8,9},{9,10... | collective-permute-start | bytes 1572872 | tf_op jit(solution)/shard_map/ppermute | solution.py:25
  186.8 23.8 %collective-permute-start.5 = (bf16[1,128,2048]{2,1,0:T(8,128)(2,1)}, bf16[1,128,2048]{2,1,0:T(8,128)(2,1)S(1)}, u32[]{:S(2)}, u32[]{:S(2)}) collective-permute-start(bf16[1,128,2048]{2,1,0:T(8,128)(2,1)} %copy.41), channel_id=1, source_target_pairs={{1,0},{2,1},{3,2},{4,3},{5,4},{6,5},{7,6},{8,7},{9,8},{10,9},{11,1... | collective-permute-start | bytes 1572872 | tf_op jit(solution)/shard_map/ppermute | solution.py:25
  190.6 25.5 %collective-permute-start.8 = (bf16[1,128,1024]{2,1,0:T(8,128)(2,1)S(1)}, bf16[1,128,1024]{2,1,0:T(8,128)(2,1)S(1)}, u32[]{:S(2)}, u32[]{:S(2)}) collective-permute-start(bf16[1,128,1024]{2,1,0:T(8,128)(2,1)S(1)} %get-tuple-element.15), channel_id=1, source_target_pairs={{1,0},{2,1},{3,2},{4,3},{5,4},{6,5},{7,6},{8,7},{9,8},{10,9},{11,1... | collective-permute-start | bytes 786440 | tf_op jit(solution)/shard_map/ppermute | solution.py:25
  192.5 29.2 %collective-permute-start.9 = (bf16[1,128,1024]{2,1,0:T(8,128)(2,1)S(1)}, bf16[1,128,1024]{2,1,0:T(8,128)(2,1)S(1)}, u32[]{:S(2)}, u32[]{:S(2)}) collective-permute-start(bf16[1,128,1024]{2,1,0:T(8,128)(2,1)S(1)} %get-tuple-element.14), channel_id=1, source_target_pairs={{1,0},{2,1},{3,2},{4,3},{5,4},{6,5},{7,6},{8,7},{9,8},{10,9},{11,1... | collective-permute-start | bytes 786440 | tf_op jit(solution)/shard_map/ppermute | solution.py:25
where the time goes:
time: 227 us; the launch traced here: 226 us
  waiting for transfers between devices  120 us (53%)
  starting transfers between devices  58.3 us (26%)
  local copies, waits for them, and re-layouts  22.7 us (10%)
  matrix products  17.6 us (8%)
  other arithmetic  6.8 us (3%)
    ppermute x6, waiting for transfers between devices, from_behind(): lax.ppermute(value, axis, [(source, source + steps) for source in range(i...  92.2 us
    ppermute x4, starting transfers between devices, shifted(): return lax.ppermute(block, axis, route)  42.4 us
    ppermute x4, waiting for transfers between devices, shifted(): return lax.ppermute(block, axis, route)  27.3 us
    ppermute x6, starting transfers between devices, from_behind(): lax.ppermute(value, axis, [(source, source + steps) for source in range(i...  15.9 us
    unnamed x23, local copies, waits for them, and re-layouts  8.47 us
    sub x2, matrix products, masked_probs(): weights = jnp.exp(scores - highest)  6.88 us
  transfers between devices with their start and end apart: 10, of which 6 were waited for; matrix products, arithmetic and copies ran while one was open for 9% of the time, Pallas kernels for 0%

commit v1 on v0

v1 whole, which is shorter than its diff:
```python
import functools

import jax
import jax.numpy as jnp
from jax import lax
from jax.experimental import pallas as pl
from jax.experimental.pallas import tpu as pltpu
from jax.sharding import PartitionSpec as P

HEAD_DIM = 128
WINDOW = 256
ROWS = 128
COLUMNS = 4
PIECE = ROWS // COLUMNS
MESH = pl.DeviceIdType.MESH

score_scale = 168.0 ** (-0.5)
masked_score = -1e30

CHUNKS = ((1, 0), (1, 1), (0, 0), (0, 1))


def last_last(a, b):
    return lax.dot_general(a, b, (((1,), (1,)), ((), ())), preferred_element_type=jnp.float32)


def first_first(a, b):
    return lax.dot_general(a, b, (((0,), (0,)), ((), ())), preferred_element_type=jnp.float32)


def kernel(
    tops,
    sections,
    kv_heads,
    q_ref,
    k_ref,
    v_ref,
    do_ref,
    seg_ref,
    att_out,
    dq_out,
    dk_out,
    dv_out,
    span,
    bias,
    att,
    dq,
    near,
    far,
    own,
    mate_near,
    got,
    final,
    rel_a,
    rel_b,
    back_a,
    back_b,
    loc_sem,
    r_send,
    r_recv,
    a_send,
    a_recv,
    b_send,
    b_recv,
    c_send,
    c_recv,
    e_send,
    e_recv,
    f_send,
    f_recv,
    g_send,
    g_recv,
    ba_send,
    ba_recv,
    bb_send,
    bb_recv,
    bc_send,
    bc_recv,
    s_send,
    s_recv,
):
    me = lax.axis_index("seq")
    sec = lax.axis_index("section")
    core = lax.rem(me, 2)
    y = lax.rem(lax.div(me, 2), COLUMNS)
    top = lax.div(me, 2 * COLUMNS)
    last = COLUMNS - 1

    def at(top_of, y_of):
        return ((top_of * COLUMNS + y_of) * 2 + core, sec)

    mate = (me + 1 - 2 * core, sec)
    after = (me, lax.rem(sec + 1, sections))
    before = (me, lax.rem(sec + sections - 1, sections))
    has_next = top < tops - 1
    has_prev = top > 0

    def copy(src, dst, send, recv, device):
        return pltpu.make_async_remote_copy(
            src_ref=src,
            dst_ref=dst,
            send_sem=send,
            recv_sem=recv,
            device_id=device,
            device_id_type=MESH,
        )

    def arrived(dst, recv):
        copy(dst, dst, e_send.at[0], recv, mate).wait_recv()

    def sent(src, send):
        copy(src, src, send, e_recv.at[0], mate).wait_send()

    sources = (k_ref, v_ref)

    def piece(q):
        return pl.ds(q * PIECE, PIECE)

    @pl.when(me == 0)
    def _():
        span[:, :, 0:WINDOW, :] = jnp.zeros((2, 2, WINDOW, span.shape[3]), span.dtype)

    @pl.when(me == 1)
    def _():
        span[:, :, 0:ROWS, :] = jnp.zeros((2, 2, ROWS, span.shape[3]), span.dtype)

    @pl.when(me >= tops * 2 * COLUMNS - 2)
    def _():
        got[...] = jnp.zeros_like(got)

    for c, (m, kv) in enumerate(CHUNKS):
        pltpu.make_async_copy(
            sources[kv].at[m], span.at[kv, m, pl.ds(WINDOW, ROWS)], loc_sem.at[c]
        ).start()

    barrier = pltpu.get_barrier_semaphore()
    pl.semaphore_signal(barrier, inc=1, device_id=mate, device_id_type=MESH)
    pl.semaphore_signal(barrier, inc=1, device_id=after, device_id_type=MESH)
    pl.semaphore_signal(barrier, inc=1, device_id=before, device_id_type=MESH)
    for step in range(1, COLUMNS):
        pl.semaphore_signal(
            barrier,
            inc=1,
            device_id=at(top, lax.rem(y + step, COLUMNS)),
            device_id_type=MESH,
        )

    for step in (1, tops - 1):
        pl.semaphore_signal(
            barrier, inc=1, device_id=at(lax.rem(top + step, tops), y), device_id_type=MESH
        )

    column_of = lax.broadcasted_iota(jnp.int32, (ROWS, ROWS), 1)
    row_of = lax.broadcasted_iota(jnp.int32, (ROWS, ROWS), 0)
    for m in range(2):
        here = pl.ds(pl.multiple_of(me * ROWS, ROWS), ROWS)
        seg_query = jnp.broadcast_to(seg_ref[m : m + 1, here].astype(jnp.float32), (ROWS, ROWS))
        for part in range(3):
            block = jnp.maximum(me - 2 + part, 0)
            there = pl.ds(pl.multiple_of(block * ROWS, ROWS), ROWS)
            seg_key = jnp.broadcast_to(seg_ref[m : m + 1, there].astype(jnp.float32), (ROWS, ROWS)).T
            offset = column_of + WINDOW - part * ROWS - row_of
            allowed = (seg_query == seg_key) & (offset >= 0) & (offset < WINDOW)
            allowed = allowed & (row_of + (part - 2 + me) * ROWS >= 0)
            value = jnp.where(allowed, 0.0, masked_score)
            bias[m, part * ROWS : (part + 1) * ROWS, 0:ROWS] = value
            bias[m, part * ROWS : (part + 1) * ROWS, ROWS : 2 * ROWS] = value

    pl.semaphore_wait(barrier, 3 + COLUMNS - 1 + 2)

    def halo_b(c, src):
        m, kv = CHUNKS[c]

        @pl.when(y == 0)
        def _():
            copy(src, span.at[kv, m, piece(0)], b_send.at[c], b_recv.at[c], at(top + 1, y)).start()

        @pl.when(y > 0)
        def _():
            copy(src, rel_b.at[c], b_send.at[c], b_recv.at[c], at(top + 1, y)).start()

    crossing = (y == last) & has_next
    for c, (m, kv) in enumerate(CHUNKS):
        source = sources[kv].at[m]

        @pl.when(crossing)
        def _():
            for q in range(last):
                copy(
                    source.at[piece(q)], rel_a.at[c], a_send.at[c, q], a_recv.at[c], at(top, q)
                ).start()
            copy(
                source.at[piece(last)], rel_b.at[c], b_send.at[c], b_recv.at[c], at(top + 1, last)
            ).start()

        @pl.when(y < last)
        def _():
            copy(
                source,
                span.at[kv, m, pl.ds(0, ROWS)],
                r_send.at[c],
                r_recv.at[c],
                at(top, y + 1),
            ).start()

        @pl.when(core == 0)
        def _():
            copy(
                source, span.at[kv, m, pl.ds(ROWS, ROWS)], e_send.at[c], e_recv.at[c], mate
            ).start()

    def relay_b(c):
        @pl.when((y < last) & has_next)
        def _():
            arrived(rel_a.at[c], a_recv.at[c])
            halo_b(c, rel_a.at[c])

    def relay_c(c):
        m, kv = CHUNKS[c]

        @pl.when((y > 0) & has_prev)
        def _():
            arrived(rel_b.at[c], b_recv.at[c])
            for q in range(1, COLUMNS):

                @pl.when(y == q)
                def _():
                    copy(
                        rel_b.at[c],
                        span.at[kv, m, piece(q)],
                        c_send.at[c],
                        c_recv.at[c, q],
                        at(top, 0),
                    ).start()

        @pl.when((y == 0) & has_prev)
        def _():
            arrived(span.at[kv, m, piece(0)], b_recv.at[c])
            for q in range(1, COLUMNS):
                arrived(span.at[kv, m, piece(q)], c_recv.at[c, q])

        @pl.when(y > 0)
        def _():
            arrived(span.at[kv, m, pl.ds(0, ROWS)], r_recv.at[c])

        @pl.when((core == 1) & (me >= 2))
        def _():
            copy(
                span.at[kv, m, pl.ds(0, ROWS)],
                span.at[kv, m, pl.ds(ROWS, ROWS)],
                e_send.at[c],
                e_recv.at[c],
                mate,
            ).start()

    def span_ready(c):
        m, kv = CHUNKS[c]

        @pl.when(me > 0)
        def _():
            arrived(span.at[kv, m, pl.ds(ROWS, ROWS)], e_recv.at[c])

        pltpu.make_async_copy(
            sources[kv].at[m], span.at[kv, m, pl.ds(WINDOW, ROWS)], loc_sem.at[c]
        ).wait()

    def pair_of(ref, index, g):
        first = pl.multiple_of(g * 2 * HEAD_DIM, HEAD_DIM)
        second = pl.multiple_of(g * 2 * HEAD_DIM + HEAD_DIM, HEAD_DIM)
        return jnp.concatenate(
            [
                ref[index + (slice(None), pl.ds(first, HEAD_DIM))],
                ref[index + (slice(None), pl.ds(second, HEAD_DIM))],
            ],
            axis=0,
        )

    def store_pair(ref, g, value):
        first = pl.multiple_of(g * 2 * HEAD_DIM, HEAD_DIM)
        second = pl.multiple_of(g * 2 * HEAD_DIM + HEAD_DIM, HEAD_DIM)
        ref[:, pl.ds(first, HEAD_DIM)] = value[:ROWS].astype(ref.dtype)
        ref[:, pl.ds(second, HEAD_DIM)] = value[ROWS:].astype(ref.dtype)

    def probs_of(m, g):
        columns = pl.ds(pl.multiple_of(g * HEAD_DIM, HEAD_DIM), HEAD_DIM)
        keys = span[0, m, :, columns]
        values = span[1, m, :, columns]
        queries = pair_of(q_ref, (m,), g)
        scores = last_last(keys, queries) * score_scale + bias[m]
        weights = jnp.exp(scores - jnp.max(scores, axis=0, keepdims=True))
        probs = weights * (1.0 / jnp.sum(weights, axis=0, keepdims=True))
        return keys, values, queries, probs

    def backward(g, carry):
        keys, values, queries, probs = probs_of(1, g)
        columns = pl.ds(pl.multiple_of(g * HEAD_DIM, HEAD_DIM), HEAD_DIM)
        grads = pair_of(do_ref, (), g)
        half = probs.astype(jnp.bfloat16)
        grad_probs = last_last(values, grads)
        delta = jnp.sum(probs * grad_probs, axis=0, keepdims=True)
        grad_scores = (probs * score_scale * (grad_probs - delta)).astype(jnp.bfloat16)
        store_pair(dq, g, first_first(grad_scores, keys))
        for kv, terms in enumerate(
            (
                jnp.dot(grad_scores, queries, preferred_element_type=jnp.float32),
                jnp.dot(half, grads, preferred_element_type=jnp.float32),
            )
        ):
            far[kv, :, columns] = terms[0:ROWS].astype(jnp.bfloat16)
            near[kv, :, columns] = terms[ROWS:WINDOW].astype(jnp.bfloat16)
            own[kv, :, columns] = terms[WINDOW:]
        return carry

    def forward(g, carry):
        _, values, _, probs = probs_of(0, g)
        store_pair(att, g, first_first(probs.astype(jnp.bfloat16), values))
        return carry

    for c in range(4):
        relay_b(c)
    for c in range(2):
        relay_c(c)
    for c in range(2):
        span_ready(c)
    lax.fori_loop(0, kv_heads, backward, 0)

    for kv in range(2):
        copy(near.at[kv], mate_near.at[kv], f_send.at[kv], f_recv.at[kv], mate).start()
    copy(dq, dq_out, s_send.at[1], s_recv.at[1], before).start()
    for c in range(2, 4):
        relay_c(c)

    back_crossing = (y == 0) & has_prev

    def back_b_send(kv, src):
        @pl.when(y == last)
        def _():
            copy(
                src, got.at[kv, piece(last)], bb_send.at[kv], bb_recv.at[kv], at(top - 1, y)
            ).start()

        @pl.when(y < last)
        def _():
            copy(src, back_b.at[kv], bb_send.at[kv], bb_recv.at[kv], at(top - 1, y)).start()

    for kv in range(2):
        arrived(mate_near.at[kv], f_recv.at[kv])

        @pl.when(core == 1)
        def _():
            far[kv] = (
                far[kv].astype(jnp.float32) + mate_near[kv].astype(jnp.float32)
            ).astype(jnp.bfloat16)

        @pl.when(y > 0)
        def _():
            copy(far.at[kv], got.at[kv], g_send.at[kv], g_recv.at[kv], at(top, y - 1)).start()

        @pl.when(back_crossing)
        def _():
            for q in range(1, COLUMNS):
                copy(
                    far.at[kv, piece(q)],
                    back_a.at[kv],
                    ba_send.at[kv, q],
                    ba_recv.at[kv],
                    at(top, q),
                ).start()
            copy(
                far.at[kv, piece(0)], back_b.at[kv], bb_send.at[kv], bb_recv.at[kv], at(top - 1, 0)
            ).start()

    for kv in range(2):

        @pl.when((y > 0) & has_prev)
        def _():
            arrived(back_a.at[kv], ba_recv.at[kv])
            back_b_send(kv, back_a.at[kv])

    for c in range(2, 4):
        span_ready(c)
    lax.fori_loop(0, kv_heads, forward, 0)
    copy(att, att_out, s_send.at[0], s_recv.at[0], after).start()

    for kv in range(2):

        @pl.when((y < last) & has_next)
        def _():
            arrived(back_b.at[kv], bb_recv.at[kv])
            for q in range(last):

                @pl.when(y == q)
                def _():
                    copy(
                        back_b.at[kv],
                        got.at[kv, piece(q)],
                        bc_send.at[kv],
                        bc_recv.at[kv, q],
                        at(top, last),
                    ).start()

    outs = (dk_out, dv_out)
    for kv in range(2):

        @pl.when(y < last)
        def _():
            arrived(got.at[kv], g_recv.at[kv])

        @pl.when((y == last) & has_next)
        def _():
            arrived(got.at[kv, piece(last)], bb_recv.at[kv])
            for q in range(last):
                arrived(got.at[kv, piece(q)], bc_recv.at[kv, q])

        @pl.when(core == 0)
        def _():
            final[kv] = (
                own[kv] + mate_near[kv].astype(jnp.float32) + got[kv].astype(jnp.float32)
            ).astype(jnp.bfloat16)

        @pl.when(core == 1)
        def _():
            final[kv] = (own[kv] + got[kv].astype(jnp.float32)).astype(jnp.bfloat16)

        copy(final.at[kv], outs[kv], s_send.at[2 + kv], s_recv.at[2 + kv], before).start()

    for c, (m, kv) in enumerate(CHUNKS):
        source = sources[kv].at[m]

        @pl.when(crossing)
        def _():
            for q in range(last):
                sent(source.at[piece(q)], a_send.at[c, q])

        @pl.when(has_next)
        def _():
            sent(rel_a.at[c], b_send.at[c])

        @pl.when(y < last)
        def _():
            sent(source, r_send.at[c])

        @pl.when((y > 0) & has_prev)
        def _():
            sent(rel_b.at[c], c_send.at[c])

        @pl.when((core == 0) | (me >= 2))
        def _():
            sent(source, e_send.at[c])

    for kv in range(2):
        sent(near.at[kv], f_send.at[kv])

        @pl.when(y > 0)
        def _():
            sent(far.at[kv], g_send.at[kv])

        @pl.when(back_crossing)
        def _():
            for q in range(1, COLUMNS):
                sent(far.at[kv, piece(q)], ba_send.at[kv, q])

        @pl.when(has_prev)
        def _():
            sent(back_a.at[kv], bb_send.at[kv])

        @pl.when((y < last) & has_next)
        def _():
            sent(back_b.at[kv], bc_send.at[kv])

    for i, (src, dst) in enumerate(
        ((att, att_out), (dq, dq_out), (final.at[0], dk_out), (final.at[1], dv_out))
    ):
        sent(src, s_send.at[i])
        arrived(dst, s_recv.at[i])


def shards(tops, sections, queries, keys, values, out_grad, segments):
    q_width = queries.shape[-1]
    k_width = keys.shape[-1]
    kv_heads = k_width // HEAD_DIM
    half, full = jnp.bfloat16, jnp.float32
    vmem = pl.BlockSpec(memory_space=pltpu.VMEM)
    hbm = pl.BlockSpec(memory_space=pl.ANY)
    dma = pltpu.SemaphoreType.DMA
    pair_sems = [dma((2,))] * 2
    results = pl.pallas_call(
        functools.partial(kernel, tops, sections, kv_heads),
        out_shape=[
            jax.ShapeDtypeStruct((ROWS, q_width), half),
            jax.ShapeDtypeStruct((ROWS, q_width), half),
            jax.ShapeDtypeStruct((ROWS, k_width), half),
            jax.ShapeDtypeStruct((ROWS, k_width), half),
        ],
        in_specs=[vmem, hbm, hbm, vmem, vmem],
        out_specs=[hbm] * 4,
        scratch_shapes=[
            pltpu.VMEM((2, 2, WINDOW + ROWS, k_width), half),
            pltpu.VMEM((2, WINDOW + ROWS, 2 * ROWS), full),
            pltpu.VMEM((ROWS, q_width), half),
            pltpu.VMEM((ROWS, q_width), half),
            pltpu.VMEM((2, ROWS, k_width), half),
            pltpu.VMEM((2, ROWS, k_width), half),
            pltpu.VMEM((2, ROWS, k_width), full),
            pltpu.VMEM((2, ROWS, k_width), half),
            pltpu.VMEM((2, ROWS, k_width), half),
            pltpu.VMEM((2, ROWS, k_width), half),
            pltpu.VMEM((4, PIECE, k_width), half),
            pltpu.VMEM((4, PIECE, k_width), half),
            pltpu.VMEM((2, PIECE, k_width), half),
            pltpu.VMEM((2, PIECE, k_width), half),
            dma((4,)),
            dma((4,)),
            dma((4,)),
            dma((4, COLUMNS)),
            dma((4,)),
            dma((4,)),
            dma((4,)),
            dma((4,)),
            dma((4, COLUMNS)),
            dma((4,)),
            dma((4,)),
            *pair_sems,
            *pair_sems,
            dma((2, COLUMNS)),
            dma((2,)),
            *pair_sems,
            dma((2,)),
            dma((2, COLUMNS)),
            dma((4,)),
            dma((4,)),
        ],
        compiler_params=pltpu.CompilerParams(collective_id=0, has_side_effects=True),
    )(queries[0], keys[0], values[0], out_grad[0], segments)
    return tuple(result[None] for result in results)


def solution(mesh):
    tops = mesh.shape["seq"] // (2 * COLUMNS)
    sections = mesh.shape["section"]
    return jax.shard_map(
        functools.partial(shards, tops, sections),
        mesh=mesh,
        in_specs=(
            P("section", None, "seq", None),
            P("section", None, "seq", None),
            P("section", None, "seq", None),
            P("section", "seq", None),
            P(),
        ),
        out_specs=(
            P("section", "seq", None),
            P("section", "seq", None),
            P("section", "seq", None),
            P("section", "seq", None),
        ),
        check_vma=False,
    )
```

time: 227 us -> 95.8 us (0.42)
  the two profiles are of different devices: /device:TPU:199 before, /device:TPU:38 now
where the time goes in v1:
time: 95.8 us; the launch traced here: 95.6 us
  Pallas kernels  90.2 us (94%)
  local copies, waits for them, and re-layouts  4.78 us (5%)
    pallas_call x1, Pallas kernels, shards(): pl.pallas_call(functools.partial(kernel, tops, sections, kv_heads), out_s...  90.2 us
    unnamed x10, local copies, waits for them, and re-layouts  4.78 us

profile of v1, /device:TPU:38, one launch (start us, length us, event | category | flops | bytes accessed | tf_op | source)
XLA Modules:
  0.0 95.6 jit_solution(18361771715963669387)
XLA Ops:
  0.6 90.2 %shard_map.84 = (bf16[128,2048]{1,0:T(8,128)(2,1)}, bf16[128,2048]{1,0:T(8,128)(2,1)}, bf16[128,1024]{1,0:T(8,128)(2,1)}, bf16[128,1024]{1,0:T(8,128)(2,1)}) custom-call(bf16[2,128,2048]{2,1,0:T(8,128)(2,1)} %bitcast.8, bf16[2,128,1024]{2,1,0:T(8,128)(2,1)} %bitcast.11, bf16[2,128,1024]{2,1,0:T(8,128)(2,1)} %bitcast.12, bf16[128,2048]{1,0:T(8,128)(2,1)} %bitcast.13, ...), custom_call_target="tpu_custom_call" | custom-call | tf_op jit(solution)/shard_map/pallas_call | solution.py:487
  90.8 0.0 copy-start
  90.8 1.9 %copy.13 = bf16[1,128,2048]{2,1,0:T(8,128)(2,1)} copy(bf16[1,128,2048]{2,1,0:T(8,128)(2,1)} %bitcast.10) | data formatting | bytes 1048576
  92.8 0.0 copy-done
  92.8 0.0 copy-start.2
  92.8 0.8 copy.14
  93.6 0.3 copy-done.2
  93.9 0.0 copy-start.1
  93.9 0.7 copy.15
  94.6 0.3 copy-done.1
  94.9 0.7 copy.16
Async XLA Ops:
  90.8 2.0 %copy-start = (bf16[128,2048]{1,0:T(8,128)(2,1)S(1)}, bf16[128,2048]{1,0:T(8,128)(2,1)}, u32[]{:S(2)}) copy-start(bf16[128,2048]{1,0:T(8,128)(2,1)} %get-tuple-element.9) | copy-start | bytes 1572868
  92.8 1.1 %copy-start.2 = (bf16[128,1024]{1,0:T(8,128)(2,1)S(1)}, bf16[128,1024]{1,0:T(8,128)(2,1)}, u32[]{:S(2)}) copy-start(bf16[128,1024]{1,0:T(8,128)(2,1)} %get-tuple-element.10) | copy-start | bytes 786436
  93.9 1.0 %copy-start.1 = (bf16[128,1024]{1,0:T(8,128)(2,1)S(1)}, bf16[128,1024]{1,0:T(8,128)(2,1)}, u32[]{:S(2)}) copy-start(bf16[128,1024]{1,0:T(8,128)(2,1)} %get-tuple-element.11) | copy-start | bytes 786436

commit v2 on v1

--- a/solution.py
+++ b/solution.py
@@ -17,7 +17,8 @@
 score_scale = 168.0 ** (-0.5)
 masked_score = -1e30
 
-CHUNKS = ((1, 0), (1, 1), (0, 0), (0, 1))
+CHUNKS = tuple((m, h, kv) for m in (1, 0) for h in range(2) for kv in range(2))
+TERMS = tuple((h, kv) for h in range(2) for kv in range(2))
 
 
 def last_last(a, b):
@@ -112,9 +113,32 @@
         copy(src, src, send, e_recv.at[0], mate).wait_send()
 
     sources = (k_ref, v_ref)
+    wide = k_ref.shape[-1] // 2
+    all_rows = pl.ds(0, ROWS)
+    near_rows = pl.ds(ROWS, ROWS)
 
     def piece(q):
         return pl.ds(q * PIECE, PIECE)
+
+    def half(h):
+        return pl.ds(h * wide, wide)
+
+    def source(c, rows):
+        m, h, kv = CHUNKS[c]
+        return sources[kv].at[m, rows, half(h)]
+
+    def spot(c, rows):
+        m, h, kv = CHUNKS[c]
+        return span.at[kv, m, rows, half(h)]
+
+    def terms_at(ref, t, rows):
+        h, kv = TERMS[t]
+        return ref.at[kv, rows, half(h)]
+
+    def loads(m, kv):
+        return pltpu.make_async_copy(
+            sources[kv].at[m], span.at[kv, m, pl.ds(WINDOW, ROWS)], loc_sem.at[m * 2 + kv]
+        )
 
     @pl.when(me == 0)
     def _():
@@ -128,10 +152,9 @@
     def _():
         got[...] = jnp.zeros_like(got)
 
-    for c, (m, kv) in enumerate(CHUNKS):
-        pltpu.make_async_copy(
-            sources[kv].at[m], span.at[kv, m, pl.ds(WINDOW, ROWS)], loc_sem.at[c]
-        ).start()
+    for m in (1, 0):
+        for kv in range(2):
+            loads(m, kv).start()
 
     barrier = pltpu.get_barrier_semaphore()
     pl.semaphore_signal(barrier, inc=1, device_id=mate, device_id_type=MESH)
@@ -169,44 +192,37 @@
     pl.semaphore_wait(barrier, 3 + COLUMNS - 1 + 2)
 
     def halo_b(c, src):
-        m, kv = CHUNKS[c]
-
         @pl.when(y == 0)
         def _():
-            copy(src, span.at[kv, m, piece(0)], b_send.at[c], b_recv.at[c], at(top + 1, y)).start()
+            copy(src, spot(c, piece(0)), b_send.at[c], b_recv.at[c], at(top + 1, y)).start()
 
         @pl.when(y > 0)
         def _():
             copy(src, rel_b.at[c], b_send.at[c], b_recv.at[c], at(top + 1, y)).start()
 
     crossing = (y == last) & has_next
-    for c, (m, kv) in enumerate(CHUNKS):
-        source = sources[kv].at[m]
+    for c in range(len(CHUNKS)):
 
         @pl.when(crossing)
         def _():
             for q in range(last):
                 copy(
-                    source.at[piece(q)], rel_a.at[c], a_send.at[c, q], a_recv.at[c], at(top, q)
+                    source(c, piece(q)), rel_a.at[c], a_send.at[c, q], a_recv.at[c], at(top, q)
                 ).start()
             copy(
-                source.at[piece(last)], rel_b.at[c], b_send.at[c], b_recv.at[c], at(top + 1, last)
+                source(c, piece(last)), rel_b.at[c], b_send.at[c], b_recv.at[c], at(top + 1, last)
             ).start()
 
         @pl.when(y < last)
         def _():
             copy(
-                source,
-                span.at[kv, m, pl.ds(0, ROWS)],
-                r_send.at[c],
-                r_recv.at[c],
-                at(top, y + 1),
+                source(c, all_rows), spot(c, all_rows), r_send.at[c], r_recv.at[c], at(top, y + 1)
             ).start()
 
         @pl.when(core == 0)
         def _():
             copy(
-                source, span.at[kv, m, pl.ds(ROWS, ROWS)], e_send.at[c], e_recv.at[c], mate
+                source(c, all_rows), spot(c, near_rows), e_send.at[c], e_recv.at[c], mate
             ).start()
 
     def relay_b(c):
@@ -216,8 +232,6 @@
             halo_b(c, rel_a.at[c])
 
     def relay_c(c):
-        m, kv = CHUNKS[c]
-
         @pl.when((y > 0) & has_prev)
         def _():
             arrived(rel_b.at[c], b_recv.at[c])
@@ -226,43 +240,35 @@
                 @pl.when(y == q)
                 def _():
                     copy(
-                        rel_b.at[c],
-                        span.at[kv, m, piece(q)],
-                        c_send.at[c],
-                        c_recv.at[c, q],
-                        at(top, 0),
+                        rel_b.at[c], spot(c, piece(q)), c_send.at[c], c_recv.at[c, q], at(top, 0)
                     ).start()
 
+    def pass_on(c):
         @pl.when((y == 0) & has_prev)
         def _():
-            arrived(span.at[kv, m, piece(0)], b_recv.at[c])
+            arrived(spot(c, piece(0)), b_recv.at[c])
             for q in range(1, COLUMNS):
-                arrived(span.at[kv, m, piece(q)], c_recv.at[c, q])
+                arrived(spot(c, piece(q)), c_recv.at[c, q])
 
         @pl.when(y > 0)
         def _():
-            arrived(span.at[kv, m, pl.ds(0, ROWS)], r_recv.at[c])
+            arrived(spot(c, all_rows), r_recv.at[c])
 
         @pl.when((core == 1) & (me >= 2))
         def _():
             copy(
-                span.at[kv, m, pl.ds(0, ROWS)],
-                span.at[kv, m, pl.ds(ROWS, ROWS)],
-                e_send.at[c],
-                e_recv.at[c],
-                mate,
+                spot(c, all_rows), spot(c, near_rows), e_send.at[c], e_recv.at[c], mate
             ).start()
 
     def span_ready(c):
-        m, kv = CHUNKS[c]
+        m, h, kv = CHUNKS[c]
 
         @pl.when(me > 0)
         def _():
-            arrived(span.at[kv, m, pl.ds(ROWS, ROWS)], e_recv.at[c])
-
-        pltpu.make_async_copy(
-            sources[kv].at[m], span.at[kv, m, pl.ds(WINDOW, ROWS)], loc_sem.at[c]
-        ).wait()
+            arrived(spot(c, near_rows), e_recv.at[c])
+
+        if h == 0:
+            loads(m, kv).wait()
 
     def pair_of(ref, index, g):
         first = pl.multiple_of(g * 2 * HEAD_DIM, HEAD_DIM)
@@ -295,7 +301,7 @@
         keys, values, queries, probs = probs_of(1, g)
         columns = pl.ds(pl.multiple_of(g * HEAD_DIM, HEAD_DIM), HEAD_DIM)
         grads = pair_of(do_ref, (), g)
-        half = probs.astype(jnp.bfloat16)
+        rounded = probs.astype(jnp.bfloat16)
         grad_probs = last_last(values, grads)
         delta = jnp.sum(probs * grad_probs, axis=0, keepdims=True)
         grad_scores = (probs * score_scale * (grad_probs - delta)).astype(jnp.bfloat16)
@@ -303,7 +309,7 @@
         for kv, terms in enumerate(
             (
                 jnp.dot(grad_scores, queries, preferred_element_type=jnp.float32),
-                jnp.dot(half, grads, preferred_element_type=jnp.float32),
+                jnp.dot(rounded, grads, preferred_element_type=jnp.float32),
             )
         ):
             far[kv, :, columns] = terms[0:ROWS].astype(jnp.bfloat16)
@@ -316,121 +322,201 @@
         store_pair(att, g, first_first(probs.astype(jnp.bfloat16), values))
         return carry
 
-    for c in range(4):
-        relay_b(c)
-    for c in range(2):
-        relay_c(c)
-    for c in range(2):
-        span_ready(c)
-    lax.fori_loop(0, kv_heads, backward, 0)
-
-    for kv in range(2):
-        copy(near.at[kv], mate_near.at[kv], f_send.at[kv], f_recv.at[kv], mate).start()
-    copy(dq, dq_out, s_send.at[1], s_recv.at[1], before).start()
-    for c in range(2, 4):
-        relay_c(c)
+    q_wide = q_ref.shape[-1] // 2
+    half_heads = kv_heads // 2
+
+    def q_half(ref, h):
+        return ref.at[:, pl.ds(h * q_wide, q_wide)]
+
+    def send_near(h):
+        for kv in range(2):
+            t = h * 2 + kv
+            copy(
+                terms_at(near, t, all_rows),
+                terms_at(mate_near, t, all_rows),
+                f_send.at[t],
+                f_recv.at[t],
+                mate,
+            ).start()
+
+    def send_queries(h):
+        copy(q_half(dq, h), q_half(dq_out, h), s_send.at[2 + h], s_recv.at[2 + h], before).start()
+
+    def send_attended(h):
+        copy(q_half(att, h), q_half(att_out, h), s_send.at[h], s_recv.at[h], after).start()
 
     back_crossing = (y == 0) & has_prev
 
-    def back_b_send(kv, src):
-        @pl.when(y == last)
+    def send_far(t):
+        h, kv = TERMS[t]
+        arrived(terms_at(mate_near, t, all_rows), f_recv.at[t])
+
+        @pl.when(core == 1)
+        def _():
+            lanes = slice(h * wide, (h + 1) * wide)
+            far[kv, :, lanes] = (
+                far[kv, :, lanes].astype(jnp.float32)
+                + mate_near[kv, :, lanes].astype(jnp.float32)
+            ).astype(jnp.bfloat16)
+
+        @pl.when(y > 0)
         def _():
             copy(
-                src, got.at[kv, piece(last)], bb_send.at[kv], bb_recv.at[kv], at(top - 1, y)
+                terms_at(far, t, all_rows),
+                terms_at(got, t, all_rows),
+                g_send.at[t],
+                g_recv.at[t],
+                at(top, y - 1),
             ).start()
-
-        @pl.when(y < last)
-        def _():
-            copy(src, back_b.at[kv], bb_send.at[kv], bb_recv.at[kv], at(top - 1, y)).start()
-
-    for kv in range(2):
-        arrived(mate_near.at[kv], f_recv.at[kv])
-
-        @pl.when(core == 1)
-        def _():
-            far[kv] = (
-                far[kv].astype(jnp.float32) + mate_near[kv].astype(jnp.float32)
-            ).astype(jnp.bfloat16)
-
-        @pl.when(y > 0)
-        def _():
-            copy(far.at[kv], got.at[kv], g_send.at[kv], g_recv.at[kv], at(top, y - 1)).start()
 
         @pl.when(back_crossing)
         def _():
             for q in range(1, COLUMNS):
                 copy(
-                    far.at[kv, piece(q)],
-                    back_a.at[kv],
-                    ba_send.at[kv, q],
-                    ba_recv.at[kv],
+                    terms_at(far, t, piece(q)),
+                    back_a.at[t],
+                    ba_send.at[t, q],
+                    ba_recv.at[t],
                     at(top, q),
                 ).start()
             copy(
-                far.at[kv, piece(0)], back_b.at[kv], bb_send.at[kv], bb_recv.at[kv], at(top - 1, 0)
+                terms_at(far, t, piece(0)),
+                back_b.at[t],
+                bb_send.at[t],
+                bb_recv.at[t],
+                at(top - 1, 0),
             ).start()
 
-    for kv in range(2):
-
+    def relay_back_b(t):
         @pl.when((y > 0) & has_prev)
         def _():
-            arrived(back_a.at[kv], ba_recv.at[kv])
-            back_b_send(kv, back_a.at[kv])
-
-    for c in range(2, 4):
-        span_ready(c)
-    lax.fori_loop(0, kv_heads, forward, 0)
-    copy(att, att_out, s_send.at[0], s_recv.at[0], after).start()
-
-    for kv in range(2):
-
+            arrived(back_a.at[t], ba_recv.at[t])
+
+            @pl.when(y == last)
+            def _():
+                copy(
+                    back_a.at[t],
+                    terms_at(got, t, piece(last)),
+                    bb_send.at[t],
+                    bb_recv.at[t],
+                    at(top - 1, y),
+                ).start()
+
+            @pl.when(y < last)
+            def _():
+                copy(
+                    back_a.at[t], back_b.at[t], bb_send.at[t], bb_recv.at[t], at(top - 1, y)
+                ).start()
+
+    def relay_back_c(t):
         @pl.when((y < last) & has_next)
         def _():
-            arrived(back_b.at[kv], bb_recv.at[kv])
+            arrived(back_b.at[t], bb_recv.at[t])
             for q in range(last):
 
                 @pl.when(y == q)
                 def _():
                     copy(
-                        back_b.at[kv],
-                        got.at[kv, piece(q)],
-                        bc_send.at[kv],
-                        bc_recv.at[kv, q],
+                        back_b.at[t],
+                        terms_at(got, t, piece(q)),
+                        bc_send.at[t],
+                        bc_recv.at[t, q],
                         at(top, last),
                     ).start()
 
     outs = (dk_out, dv_out)
-    for kv in range(2):
+
+    def finish(t):
+        h, kv = TERMS[t]
+        lanes = slice(h * wide, (h + 1) * wide)
 
         @pl.when(y < last)
         def _():
-            arrived(got.at[kv], g_recv.at[kv])
+            arrived(terms_at(got, t, all_rows), g_recv.at[t])
 
         @pl.when((y == last) & has_next)
         def _():
-            arrived(got.at[kv, piece(last)], bb_recv.at[kv])
+            arrived(terms_at(got, t, piece(last)), bb_recv.at[t])
             for q in range(last):
-                arrived(got.at[kv, piece(q)], bc_recv.at[kv, q])
+                arrived(terms_at(got, t, piece(q)), bc_recv.at[t, q])
+
+        total = own[kv, :, lanes] + got[kv, :, lanes].astype(jnp.float32)
 
         @pl.when(core == 0)
         def _():
-            final[kv] = (
-                own[kv] + mate_near[kv].astype(jnp.float32) + got[kv].astype(jnp.float32)
-            ).astype(jnp.bfloat16)
+            final[kv, :, lanes] = (total + mate_near[kv, :, lanes].astype(jnp.float32)).astype(
+                jnp.bfloat16
+            )
 
         @pl.when(core == 1)
         def _():
-            final[kv] = (own[kv] + got[kv].astype(jnp.float32)).astype(jnp.bfloat16)
-
-        copy(final.at[kv], outs[kv], s_send.at[2 + kv], s_recv.at[2 + kv], before).start()
-
-    for c, (m, kv) in enumerate(CHUNKS):
-        source = sources[kv].at[m]
+            final[kv, :, lanes] = total.astype(jnp.bfloat16)
+
+        copy(
+            terms_at(final, t, all_rows),
+            outs[kv].at[:, half(h)],
+            s_send.at[4 + t],
+            s_recv.at[4 + t],
+            before,
+        ).start()
+
+    for c in range(8):
+        relay_b(c)
+    for c in (0, 1):
+        relay_c(c)
+    for c in (0, 1):
+        pass_on(c)
+    for c in (0, 1):
+        span_ready(c)
+    lax.fori_loop(0, half_heads, backward, 0)
+    send_near(0)
+    send_queries(0)
+    for c in (2, 3):
+        relay_c(c)
+    for c in (2, 3):
+        pass_on(c)
+    for t in (0, 1):
+        send_far(t)
+    for c in (2, 3):
+        span_ready(c)
+    lax.fori_loop(half_heads, kv_heads, backward, 0)
+    send_near(1)
+    send_queries(1)
+    for t in (0, 1):
+        relay_back_b(t)
+    for t in (2, 3):
+        send_far(t)
+    for c in (4, 5):
+        relay_c(c)
+    for t in (2, 3):
+        relay_back_b(t)
+    for c in (6, 7):
+        relay_c(c)
+    for c in (4, 5):
+        pass_on(c)
+    for c in (4, 5):
+        span_ready(c)
+    lax.fori_loop(0, half_heads, forward, 0)
+    send_attended(0)
+    for t in (0, 1):
+        relay_back_c(t)
+    for c in (6, 7):
+        pass_on(c)
+    for c in (6, 7):
+        span_ready(c)
+    lax.fori_loop(half_heads, kv_heads, forward, 0)
+    send_attended(1)
+    for t in (2, 3):
+        relay_back_c(t)
+    for t in range(4):
+        finish(t)
+
+    for c in range(len(CHUNKS)):
 
         @pl.when(crossing)
         def _():
             for q in range(last):
-                sent(source.at[piece(q)], a_send.at[c, q])
+                sent(source(c, piece(q)), a_send.at[c, q])
 
         @pl.when(has_next)
         def _():
@@ -438,7 +524,7 @@
 
         @pl.when(y < last)
         def _():
-            sent(source, r_send.at[c])
+            sent(source(c, all_rows), r_send.at[c])
 
         @pl.when((y > 0) & has_prev)
         def _():
@@ -446,31 +532,32 @@
 
         @pl.when((core == 0) | (me >= 2))
         def _():
-            sent(source, e_send.at[c])
-
-    for kv in range(2):
-        sent(near.at[kv], f_send.at[kv])
+            sent(source(c, all_rows), e_send.at[c])
+
+    for t in range(len(TERMS)):
+        sent(terms_at(near, t, all_rows), f_send.at[t])
 
         @pl.when(y > 0)
         def _():
-            sent(far.at[kv], g_send.at[kv])
+            sent(terms_at(far, t, all_rows), g_send.at[t])
 
         @pl.when(back_crossing)
         def _():
             for q in range(1, COLUMNS):
-                sent(far.at[kv, piece(q)], ba_send.at[kv, q])
+                sent(terms_at(far, t, piece(q)), ba_send.at[t, q])
 
         @pl.when(has_prev)
         def _():
-            sent(back_a.at[kv], bb_send.at[kv])
+            sent(back_a.at[t], bb_send.at[t])
 
         @pl.when((y < last) & has_next)
         def _():
-            sent(back_b.at[kv], bc_send.at[kv])
-
-    for i, (src, dst) in enumerate(
-        ((att, att_out), (dq, dq_out), (final.at[0], dk_out), (final.at[1], dv_out))
-    ):
+            sent(back_b.at[t], bc_send.at[t])
+
+    moved = [(q_half(att, h), q_half(att_out, h)) for h in range(2)]
+    moved += [(q_half(dq, h), q_half(dq_out, h)) for h in range(2)]
+    moved += [(terms_at(final, t, all_rows), outs[t % 2].at[:, half(t // 2)]) for t in range(4)]
+    for i, (src, dst) in enumerate(moved):
         sent(src, s_send.at[i])
         arrived(dst, s_recv.at[i])
 
@@ -483,7 +570,6 @@
     vmem = pl.BlockSpec(memory_space=pltpu.VMEM)
     hbm = pl.BlockSpec(memory_space=pl.ANY)
     dma = pltpu.SemaphoreType.DMA
-    pair_sems = [dma((2,))] * 2
     results = pl.pallas_call(
         functools.partial(kernel, tops, sections, kv_heads),
         out_shape=[
@@ -505,10 +591,22 @@
             pltpu.VMEM((2, ROWS, k_width), half),
             pltpu.VMEM((2, ROWS, k_width), half),
             pltpu.VMEM((2, ROWS, k_width), half),
-            pltpu.VMEM((4, PIECE, k_width), half),
-            pltpu.VMEM((4, PIECE, k_width), half),
-            pltpu.VMEM((2, PIECE, k_width), half),
-            pltpu.VMEM((2, PIECE, k_width), half),
+            pltpu.VMEM((8, PIECE, k_width // 2), half),
+            pltpu.VMEM((8, PIECE, k_width // 2), half),
+            pltpu.VMEM((4, PIECE, k_width // 2), half),
+            pltpu.VMEM((4, PIECE, k_width // 2), half),
+            dma((4,)),
+            dma((8,)),
+            dma((8,)),
+            dma((8, COLUMNS)),
+            dma((8,)),
+            dma((8,)),
+            dma((8,)),
+            dma((8,)),
+            dma((8, COLUMNS)),
+            dma((8,)),
+            dma((8,)),
+            dma((4,)),
             dma((4,)),
             dma((4,)),
             dma((4,)),
@@ -518,17 +616,8 @@
             dma((4,)),
             dma((4,)),
             dma((4, COLUMNS)),
-            dma((4,)),
-            dma((4,)),
-            *pair_sems,
-            *pair_sems,
-            dma((2, COLUMNS)),
-            dma((2,)),
-            *pair_sems,
-            dma((2,)),
-            dma((2, COLUMNS)),
-            dma((4,)),
-            dma((4,)),
+            dma((8,)),
+            dma((8,)),
         ],
         compiler_params=pltpu.CompilerParams(collective_id=0, has_side_effects=True),
     )(queries[0], keys[0], values[0], out_grad[0], segments)

time: 95.8 us -> 91.5 us (0.955)
  the two profiles are of different devices: /device:TPU:38 before, /device:TPU:46 now
where the time goes in v2:
time: 91.5 us; the launch traced here: 91.3 us
  Pallas kernels  85.8 us (94%)
  local copies, waits for them, and re-layouts  4.78 us (5%)
    pallas_call x1, Pallas kernels, shards(): pl.pallas_call(functools.partial(kernel, tops, sections, kv_heads), out_s...  85.8 us
    unnamed x10, local copies, waits for them, and re-layouts  4.78 us

profile of v2, /device:TPU:46, one launch (start us, length us, event | category | flops | bytes accessed | tf_op | source)
XLA Modules:
  0.0 91.3 jit_solution(3583064300181242989)
XLA Ops:
  0.6 85.8 %shard_map.84 = (bf16[128,2048]{1,0:T(8,128)(2,1)}, bf16[128,2048]{1,0:T(8,128)(2,1)}, bf16[128,1024]{1,0:T(8,128)(2,1)}, bf16[128,1024]{1,0:T(8,128)(2,1)}) custom-call(bf16[2,128,2048]{2,1,0:T(8,128)(2,1)} %bitcast.8, bf16[2,128,1024]{2,1,0:T(8,128)(2,1)} %bitcast.11, bf16[2,128,1024]{2,1,0:T(8,128)(2,1)} %bitcast.12, bf16[128,2048]{1,0:T(8,128)(2,1)} %bitcast.13, ...), custom_call_target="tpu_custom_call" | custom-call | tf_op jit(solution)/shard_map/pallas_call | solution.py:573
  86.5 0.0 copy-start
  86.5 1.9 %copy.13 = bf16[1,128,2048]{2,1,0:T(8,128)(2,1)} copy(bf16[1,128,2048]{2,1,0:T(8,128)(2,1)} %bitcast.10) | data formatting | bytes 1048576
  88.4 0.0 copy-done
  88.4 0.0 copy-start.2
  88.4 0.8 copy.14
  89.2 0.3 copy-done.2
  89.5 0.0 copy-start.1
  89.5 0.7 copy.15
  90.2 0.3 copy-done.1
  90.6 0.7 copy.16
Async XLA Ops:
  86.5 2.0 %copy-start = (bf16[128,2048]{1,0:T(8,128)(2,1)S(1)}, bf16[128,2048]{1,0:T(8,128)(2,1)}, u32[]{:S(2)}) copy-start(bf16[128,2048]{1,0:T(8,128)(2,1)} %get-tuple-element.9) | copy-start | bytes 1572868
  88.4 1.1 %copy-start.2 = (bf16[128,1024]{1,0:T(8,128)(2,1)S(1)}, bf16[128,1024]{1,0:T(8,128)(2,1)}, u32[]{:S(2)}) copy-start(bf16[128,1024]{1,0:T(8,128)(2,1)} %get-tuple-element.10) | copy-start | bytes 786436
  89.5 1.0 %copy-start.1 = (bf16[128,1024]{1,0:T(8,128)(2,1)S(1)}, bf16[128,1024]{1,0:T(8,128)(2,1)}, u32[]{:S(2)}) copy-start(bf16[128,1024]{1,0:T(8,128)(2,1)} %get-tuple-element.11) | copy-start | bytes 786436

commit v3 on v2

--- a/solution.py
+++ b/solution.py
@@ -168,10 +168,14 @@
             device_id_type=MESH,
         )
 
-    for step in (1, tops - 1):
-        pl.semaphore_signal(
-            barrier, inc=1, device_id=at(lax.rem(top + step, tops), y), device_id_type=MESH
-        )
+
+    @pl.when(has_next)
+    def _():
+        pl.semaphore_signal(barrier, inc=1, device_id=at(top + 1, y), device_id_type=MESH)
+
+    @pl.when(has_prev)
+    def _():
+        pl.semaphore_signal(barrier, inc=1, device_id=at(top - 1, y), device_id_type=MESH)
 
     column_of = lax.broadcasted_iota(jnp.int32, (ROWS, ROWS), 1)
     row_of = lax.broadcasted_iota(jnp.int32, (ROWS, ROWS), 0)
@@ -189,7 +193,8 @@
             bias[m, part * ROWS : (part + 1) * ROWS, 0:ROWS] = value
             bias[m, part * ROWS : (part + 1) * ROWS, ROWS : 2 * ROWS] = value
 
-    pl.semaphore_wait(barrier, 3 + COLUMNS - 1 + 2)
+    across = jnp.minimum(top, 1) + jnp.minimum(tops - 1 - top, 1)
+    pl.semaphore_wait(barrier, 3 + COLUMNS - 1 + across)
 
     def halo_b(c, src):
         @pl.when(y == 0)
@@ -426,20 +431,26 @@
 
     outs = (dk_out, dv_out)
 
+    def finish_near(t):
+        @pl.when(y < last)
+        def _():
+            arrived(terms_at(got, t, all_rows), g_recv.at[t])
+            finish(t)
+
+    def finish_across(t):
+        @pl.when(y == last)
+        def _():
+            @pl.when(has_next)
+            def _():
+                arrived(terms_at(got, t, piece(last)), bb_recv.at[t])
+                for q in range(last):
+                    arrived(terms_at(got, t, piece(q)), bc_recv.at[t, q])
+
+            finish(t)
+
     def finish(t):
         h, kv = TERMS[t]
         lanes = slice(h * wide, (h + 1) * wide)
-
-        @pl.when(y < last)
-        def _():
-            arrived(terms_at(got, t, all_rows), g_recv.at[t])
-
-        @pl.when((y == last) & has_next)
-        def _():
-            arrived(terms_at(got, t, piece(last)), bb_recv.at[t])
-            for q in range(last):
-                arrived(terms_at(got, t, piece(q)), bc_recv.at[t, q])
-
         total = own[kv, :, lanes] + got[kv, :, lanes].astype(jnp.float32)
 
         @pl.when(core == 0)
@@ -499,6 +510,8 @@
     lax.fori_loop(0, half_heads, forward, 0)
     send_attended(0)
     for t in (0, 1):
+        finish_near(t)
+    for t in (0, 1):
         relay_back_c(t)
     for c in (6, 7):
         pass_on(c)
@@ -507,9 +520,11 @@
     lax.fori_loop(half_heads, kv_heads, forward, 0)
     send_attended(1)
     for t in (2, 3):
+        finish_near(t)
+    for t in (2, 3):
         relay_back_c(t)
     for t in range(4):
-        finish(t)
+        finish_across(t)
 
     for c in range(len(CHUNKS)):
 

time: 91.5 us -> 91.5 us (level)
  the two profiles are of different devices: /device:TPU:46 before, /device:TPU:62 now
where the time goes in v3:
time: 91.5 us; the launch traced here: 91.3 us
  Pallas kernels  85.8 us (94%)
  local copies, waits for them, and re-layouts  4.78 us (5%)
    pallas_call x1, Pallas kernels, shards(): pl.pallas_call(functools.partial(kernel, tops, sections, kv_heads), out_s...  85.8 us
    unnamed x10, local copies, waits for them, and re-layouts  4.78 us

profile of v3, /device:TPU:62, one launch (start us, length us, event | category | flops | bytes accessed | tf_op | source)
XLA Modules:
  0.0 91.3 jit_solution(952616570025950216)
XLA Ops:
  0.6 85.8 %shard_map.84 = (bf16[128,2048]{1,0:T(8,128)(2,1)}, bf16[128,2048]{1,0:T(8,128)(2,1)}, bf16[128,1024]{1,0:T(8,128)(2,1)}, bf16[128,1024]{1,0:T(8,128)(2,1)}) custom-call(bf16[2,128,2048]{2,1,0:T(8,128)(2,1)} %bitcast.8, bf16[2,128,1024]{2,1,0:T(8,128)(2,1)} %bitcast.11, bf16[2,128,1024]{2,1,0:T(8,128)(2,1)} %bitcast.12, bf16[128,2048]{1,0:T(8,128)(2,1)} %bitcast.13, ...), custom_call_target="tpu_custom_call" | custom-call | tf_op jit(solution)/shard_map/pallas_call | solution.py:588
  86.5 0.0 copy-start
  86.5 1.9 %copy.13 = bf16[1,128,2048]{2,1,0:T(8,128)(2,1)} copy(bf16[1,128,2048]{2,1,0:T(8,128)(2,1)} %bitcast.10) | data formatting | bytes 1048576
  88.4 0.0 copy-done
  88.4 0.0 copy-start.2
  88.4 0.8 copy.14
  89.2 0.3 copy-done.2
  89.5 0.0 copy-start.1
  89.5 0.7 copy.15
  90.2 0.3 copy-done.1
  90.6 0.7 copy.16
Async XLA Ops:
  86.5 2.0 %copy-start = (bf16[128,2048]{1,0:T(8,128)(2,1)S(1)}, bf16[128,2048]{1,0:T(8,128)(2,1)}, u32[]{:S(2)}) copy-start(bf16[128,2048]{1,0:T(8,128)(2,1)} %get-tuple-element.9) | copy-start | bytes 1572868
  88.4 1.1 %copy-start.2 = (bf16[128,1024]{1,0:T(8,128)(2,1)S(1)}, bf16[128,1024]{1,0:T(8,128)(2,1)}, u32[]{:S(2)}) copy-start(bf16[128,1024]{1,0:T(8,128)(2,1)} %get-tuple-element.10) | copy-start | bytes 786436
  89.5 1.0 %copy-start.1 = (bf16[128,1024]{1,0:T(8,128)(2,1)S(1)}, bf16[128,1024]{1,0:T(8,128)(2,1)}, u32[]{:S(2)}) copy-start(bf16[128,1024]{1,0:T(8,128)(2,1)} %get-tuple-element.11) | copy-start | bytes 786436

commit v4 on v3

--- a/solution.py
+++ b/solution.py
@@ -11,6 +11,7 @@
 WINDOW = 256
 ROWS = 128
 COLUMNS = 4
+SECTION_RUN = 4
 PIECE = ROWS // COLUMNS
 MESH = pl.DeviceIdType.MESH
 
@@ -93,6 +94,8 @@
     mate = (me + 1 - 2 * core, sec)
     after = (me, lax.rem(sec + 1, sections))
     before = (me, lax.rem(sec + sections - 1, sections))
+    yields_back = (lax.rem(sec, SECTION_RUN) == 0) & (sec > 0) & (y < last)
+    yields_on = sec == sections - 1
     has_next = top < tops - 1
     has_prev = top > 0
 
@@ -463,6 +466,12 @@
         def _():
             final[kv, :, lanes] = total.astype(jnp.bfloat16)
 
+        @pl.when(jnp.logical_not(yields_back))
+        def _():
+            send_terms(t)
+
+    def send_terms(t):
+        h, kv = TERMS[t]
         copy(
             terms_at(final, t, all_rows),
             outs[kv].at[:, half(h)],
@@ -492,7 +501,11 @@
         span_ready(c)
     lax.fori_loop(half_heads, kv_heads, backward, 0)
     send_near(1)
-    send_queries(1)
+
+    @pl.when(jnp.logical_not(yields_back))
+    def _():
+        send_queries(1)
+
     for t in (0, 1):
         relay_back_b(t)
     for t in (2, 3):
@@ -508,7 +521,11 @@
     for c in (4, 5):
         span_ready(c)
     lax.fori_loop(0, half_heads, forward, 0)
-    send_attended(0)
+
+    @pl.when(jnp.logical_not(yields_on))
+    def _():
+        send_attended(0)
+
     for t in (0, 1):
         finish_near(t)
     for t in (0, 1):
@@ -518,11 +535,27 @@
     for c in (6, 7):
         span_ready(c)
     lax.fori_loop(half_heads, kv_heads, forward, 0)
-    send_attended(1)
+
+    @pl.when(jnp.logical_not(yields_on))
+    def _():
+        send_attended(1)
+
     for t in (2, 3):
         finish_near(t)
     for t in (2, 3):
         relay_back_c(t)
+
+    @pl.when(yields_back)
+    def _():
+        send_queries(1)
+        for t in range(4):
+            send_terms(t)
+
+    @pl.when(yields_on)
+    def _():
+        for h in range(2):
+            send_attended(h)
+
     for t in range(4):
         finish_across(t)
 
@@ -588,10 +621,10 @@
     results = pl.pallas_call(
         functools.partial(kernel, tops, sections, kv_heads),
         out_shape=[
-            jax.ShapeDtypeStruct((ROWS, q_width), half),
-            jax.ShapeDtypeStruct((ROWS, q_width), half),
-            jax.ShapeDtypeStruct((ROWS, k_width), half),
-            jax.ShapeDtypeStruct((ROWS, k_width), half),
+            pltpu.VMEM((ROWS, q_width), half),
+            pltpu.VMEM((ROWS, q_width), half),
+            pltpu.VMEM((ROWS, k_width), half),
+            pltpu.VMEM((ROWS, k_width), half),
         ],
         in_specs=[vmem, hbm, hbm, vmem, vmem],
         out_specs=[hbm] * 4,

time: 91.5 us -> 94.6 us (1.034)
  the two profiles are of different devices: /device:TPU:62 before, /device:TPU:166 now
where the time goes in v4:
time: 94.6 us; the launch traced here: 94.5 us
  Pallas kernels  90.8 us (96%)
  local copies, waits for them, and re-layouts  2.99 us (3%)
    pallas_call x1, Pallas kernels, shards(): pl.pallas_call(functools.partial(kernel, tops, sections, kv_heads), out_s...  90.8 us
    unnamed x4, local copies, waits for them, and re-layouts  2.99 us

profile of v4, /device:TPU:166, one launch (start us, length us, event | category | flops | bytes accessed | tf_op | source)
XLA Modules:
  0.0 94.5 jit_solution(7750775038949791477)
XLA Ops:
  0.6 90.8 %shard_map.84 = (bf16[128,2048]{1,0:T(8,128)(2,1)S(1)}, bf16[128,2048]{1,0:T(8,128)(2,1)S(1)}, bf16[128,1024]{1,0:T(8,128)(2,1)S(1)}, bf16[128,1024]{1,0:T(8,128)(2,1)S(1)}) custom-call(bf16[2,128,2048]{2,1,0:T(8,128)(2,1)} %bitcast.12, bf16[2,128,1024]{2,1,0:T(8,128)(2,1)} %bitcast.13, bf16[2,128,1024]{2,1,0:T(8,128)(2,1)} %bitcast.14, ...), custom_call_target="tpu_custom_call" | custom-call | tf_op jit(solution)/shard_map/pallas_call | solution.py:621
  91.5 0.8 copy.13
  92.3 0.8 copy.14
  93.1 0.7 copy.15
  93.8 0.7 copy.16

commit v5 on v3

--- a/solution.py
+++ b/solution.py
@@ -11,6 +11,7 @@
 WINDOW = 256
 ROWS = 128
 COLUMNS = 4
+RUN = 4
 PIECE = ROWS // COLUMNS
 MESH = pl.DeviceIdType.MESH
 
@@ -79,6 +80,9 @@
     bc_recv,
     s_send,
     s_recv,
+    turned,
+    t_send,
+    t_recv,
 ):
     me = lax.axis_index("seq")
     sec = lax.axis_index("section")
@@ -93,6 +97,12 @@
     mate = (me + 1 - 2 * core, sec)
     after = (me, lax.rem(sec + 1, sections))
     before = (me, lax.rem(sec + sections - 1, sections))
+    x = lax.rem(sec, RUN)
+    low = lax.div(sec, RUN)
+    lows = sections // RUN
+    turns = (x == 0) & (low > 0)
+    corner = (x == RUN - 1) & (low > 0)
+    corner_after = (x == RUN - 1) & (low < lows - 1)
     has_next = top < tops - 1
     has_prev = top > 0
 
@@ -176,6 +186,16 @@
     @pl.when(has_prev)
     def _():
         pl.semaphore_signal(barrier, inc=1, device_id=at(top - 1, y), device_id_type=MESH)
+
+    def greet(condition, section):
+        @pl.when(condition)
+        def _():
+            pl.semaphore_signal(barrier, inc=1, device_id=(me, section), device_id_type=MESH)
+
+    greet(turns, sec + RUN - 1)
+    greet(corner, sec - RUN + 1)
+    greet(corner, sec - RUN)
+    greet(corner_after, sec + RUN)
 
     column_of = lax.broadcasted_iota(jnp.int32, (ROWS, ROWS), 1)
     row_of = lax.broadcasted_iota(jnp.int32, (ROWS, ROWS), 0)
@@ -194,7 +214,10 @@
             bias[m, part * ROWS : (part + 1) * ROWS, ROWS : 2 * ROWS] = value
 
     across = jnp.minimum(top, 1) + jnp.minimum(tops - 1 - top, 1)
-    pl.semaphore_wait(barrier, 3 + COLUMNS - 1 + across)
+    first, final_x = 1 - jnp.minimum(x, 1), jnp.maximum(x - (RUN - 2), 0)
+    behind, ahead = jnp.minimum(low, 1), jnp.minimum(lows - 1 - low, 1)
+    turning = first * behind + final_x * (2 * behind + ahead)
+    pl.semaphore_wait(barrier, 3 + COLUMNS - 1 + across + turning)
 
     def halo_b(c, src):
         @pl.when(y == 0)
@@ -345,7 +368,33 @@
             ).start()
 
     def send_queries(h):
-        copy(q_half(dq, h), q_half(dq_out, h), s_send.at[2 + h], s_recv.at[2 + h], before).start()
+        @pl.when(turns)
+        def _():
+            copy(
+                q_half(dq, h),
+                turned.at[h],
+                s_send.at[2 + h],
+                t_recv.at[h],
+                (me, sec + RUN - 1),
+            ).start()
+
+        @pl.when(jnp.logical_not(turns))
+        def _():
+            copy(
+                q_half(dq, h), q_half(dq_out, h), s_send.at[2 + h], s_recv.at[2 + h], before
+            ).start()
+
+    def turn(h):
+        @pl.when(corner)
+        def _():
+            arrived(turned.at[h], t_recv.at[h])
+            copy(
+                turned.at[h],
+                q_half(dq_out, h),
+                t_send.at[h],
+                s_recv.at[2 + h],
+                (me, sec - RUN),
+            ).start()
 
     def send_attended(h):
         copy(q_half(att, h), q_half(att_out, h), s_send.at[h], s_recv.at[h], after).start()
@@ -503,6 +552,7 @@
         relay_back_b(t)
     for c in (6, 7):
         relay_c(c)
+    turn(0)
     for c in (4, 5):
         pass_on(c)
     for c in (4, 5):
@@ -521,6 +571,7 @@
     send_attended(1)
     for t in (2, 3):
         finish_near(t)
+    turn(1)
     for t in (2, 3):
         relay_back_c(t)
     for t in range(4):
@@ -568,6 +619,11 @@
         @pl.when((y < last) & has_next)
         def _():
             sent(back_b.at[t], bc_send.at[t])
+
+    @pl.when(corner)
+    def _():
+        for h in range(2):
+            sent(turned.at[h], t_send.at[h])
 
     moved = [(q_half(att, h), q_half(att_out, h)) for h in range(2)]
     moved += [(q_half(dq, h), q_half(dq_out, h)) for h in range(2)]
@@ -588,10 +644,10 @@
     results = pl.pallas_call(
         functools.partial(kernel, tops, sections, kv_heads),
         out_shape=[
-            jax.ShapeDtypeStruct((ROWS, q_width), half),
-            jax.ShapeDtypeStruct((ROWS, q_width), half),
-            jax.ShapeDtypeStruct((ROWS, k_width), half),
-            jax.ShapeDtypeStruct((ROWS, k_width), half),
+            pltpu.VMEM((ROWS, q_width), half),
+            pltpu.VMEM((ROWS, q_width), half),
+            pltpu.VMEM((ROWS, k_width), half),
+            pltpu.VMEM((ROWS, k_width), half),
         ],
         in_specs=[vmem, hbm, hbm, vmem, vmem],
         out_specs=[hbm] * 4,
@@ -633,6 +689,9 @@
             dma((4, COLUMNS)),
             dma((8,)),
             dma((8,)),
+            pltpu.VMEM((2, ROWS, q_width // 2), half),
+            dma((2,)),
+            dma((2,)),
         ],
         compiler_params=pltpu.CompilerParams(collective_id=0, has_side_effects=True),
     )(queries[0], keys[0], values[0], out_grad[0], segments)

time: 91.5 us -> 88.4 us (0.966)
  the two profiles are of different devices: /device:TPU:62 before, /device:TPU:190 now
where the time goes in v5:
time: 88.4 us; the launch traced here: 88.2 us
  Pallas kernels  84.6 us (96%)
  local copies, waits for them, and re-layouts  2.99 us (3%)
    pallas_call x1, Pallas kernels, shards(): pl.pallas_call(functools.partial(kernel, tops, sections, kv_heads), out_s...  84.6 us
    unnamed x4, local copies, waits for them, and re-layouts  2.99 us

profile of v5, /device:TPU:190, one launch (start us, length us, event | category | flops | bytes accessed | tf_op | source)
XLA Modules:
  0.0 88.2 jit_solution(17886458760145501305)
XLA Ops:
  0.6 84.6 %shard_map.84 = (bf16[128,2048]{1,0:T(8,128)(2,1)S(1)}, bf16[128,2048]{1,0:T(8,128)(2,1)S(1)}, bf16[128,1024]{1,0:T(8,128)(2,1)S(1)}, bf16[128,1024]{1,0:T(8,128)(2,1)S(1)}) custom-call(bf16[2,128,2048]{2,1,0:T(8,128)(2,1)} %bitcast.12, bf16[2,128,1024]{2,1,0:T(8,128)(2,1)} %bitcast.13, bf16[2,128,1024]{2,1,0:T(8,128)(2,1)} %bitcast.14, ...), custom_call_target="tpu_custom_call" | custom-call | tf_op jit(solution)/shard_map/pallas_call | solution.py:644
  85.2 0.8 copy.13
  86.0 0.8 copy.14
  86.8 0.7 copy.15
  87.5 0.7 copy.16

commit v6 on v5

--- a/solution.py
+++ b/solution.py
@@ -546,10 +546,10 @@
         relay_back_b(t)
     for t in (2, 3):
         send_far(t)
+    for t in (2, 3):
+        relay_back_b(t)
     for c in (4, 5):
         relay_c(c)
-    for t in (2, 3):
-        relay_back_b(t)
     for c in (6, 7):
         relay_c(c)
     turn(0)

time: 88.4 us -> 88.4 us (level)
  no operation moved by 1% of the time
where the time goes in v6:
time: 88.4 us; the launch traced here: 88.2 us
  Pallas kernels  84.6 us (96%)
  local copies, waits for them, and re-layouts  2.99 us (3%)
    pallas_call x1, Pallas kernels, shards(): pl.pallas_call(functools.partial(kernel, tops, sections, kv_heads), out_s...  84.6 us
    unnamed x4, local copies, waits for them, and re-layouts  2.99 us

profile of v6, /device:TPU:190, one launch (start us, length us, event | category | flops | bytes accessed | tf_op | source)
XLA Modules:
  0.0 88.2 jit_solution(11150246208204397934)
XLA Ops:
  0.6 84.6 %shard_map.84 = (bf16[128,2048]{1,0:T(8,128)(2,1)S(1)}, bf16[128,2048]{1,0:T(8,128)(2,1)S(1)}, bf16[128,1024]{1,0:T(8,128)(2,1)S(1)}, bf16[128,1024]{1,0:T(8,128)(2,1)S(1)}) custom-call(bf16[2,128,2048]{2,1,0:T(8,128)(2,1)} %bitcast.12, bf16[2,128,1024]{2,1,0:T(8,128)(2,1)} %bitcast.13, bf16[2,128,1024]{2,1,0:T(8,128)(2,1)} %bitcast.14, ...), custom_call_target="tpu_custom_call" | custom-call | tf_op jit(solution)/shard_map/pallas_call | solution.py:644
  85.2 0.8 copy.13
  86.0 0.8 copy.14
  86.8 0.7 copy.15
  87.5 0.7 copy.16

commit v7 on v6

--- a/solution.py
+++ b/solution.py
@@ -520,10 +520,12 @@
             before,
         ).start()
 
-    for c in range(8):
+    for c in range(6):
         relay_b(c)
     for c in (0, 1):
         relay_c(c)
+    for c in (6, 7):
+        relay_b(c)
     for c in (0, 1):
         pass_on(c)
     for c in (0, 1):

time: 88.4 us -> 88.4 us (level)
  no operation moved by 1% of the time
where the time goes in v7:
time: 88.4 us; the launch traced here: 88.3 us
  Pallas kernels  84.6 us (96%)
  local copies, waits for them, and re-layouts  2.99 us (3%)
    pallas_call x1, Pallas kernels, shards(): pl.pallas_call(functools.partial(kernel, tops, sections, kv_heads), out_s...  84.6 us
    unnamed x4, local copies, waits for them, and re-layouts  2.99 us

profile of v7, /device:TPU:190, one launch (start us, length us, event | category | flops | bytes accessed | tf_op | source)
XLA Modules:
  0.0 88.3 jit_solution(5466877313757698195)
XLA Ops:
  0.6 84.6 %shard_map.84 = (bf16[128,2048]{1,0:T(8,128)(2,1)S(1)}, bf16[128,2048]{1,0:T(8,128)(2,1)S(1)}, bf16[128,1024]{1,0:T(8,128)(2,1)S(1)}, bf16[128,1024]{1,0:T(8,128)(2,1)S(1)}) custom-call(bf16[2,128,2048]{2,1,0:T(8,128)(2,1)} %bitcast.12, bf16[2,128,1024]{2,1,0:T(8,128)(2,1)} %bitcast.13, bf16[2,128,1024]{2,1,0:T(8,128)(2,1)} %bitcast.14, ...), custom_call_target="tpu_custom_call" | custom-call | tf_op jit(solution)/shard_map/pallas_call | solution.py:646
  85.3 0.8 copy.13
  86.1 0.8 copy.14
  86.9 0.7 copy.15
  87.6 0.7 copy.16
